TPU v7x, 128 devices: a whole 4x4x4 slice. The times are simulated.
128 devices in a mesh: lat: 8 (over z, y_hi), lon: 16 (over y_lo, x, core).
Axes of the slice: x: 4, y: 4 (y_hi: 2, y_lo: 2; y = y_hi * 2 + y_lo), z: 4, core: 2. Of those that a mesh axis runs over, the one named last changes fastest.
Arguments:
- tokens: float32 [8, 16, 512, 1024], P('lat', 'lon')
- norm_gain: float32 [1024], replicated, may hold values from 0.5 to 6, as said below
- qkv_weight: bfloat16 [1024, 3072], replicated, may hold values from -0.1875 to 0.1875
- out_weight: bfloat16 [1024, 1024], replicated, may hold values from -0.1875 to 0.1875
- band_counts: int32 [8], P('lat'), may hold values from 256 to 512, as said below
- halo_rows: int32 [8, 2, 128], replicated, may hold values from 0 to 511, as said below
- window_mask: int32 [8, 16, 4, 5], P('lat', 'lon'), may hold values from 0 to 1, as said below
Outputs:
- updated: float32 [8, 16, 512, 1024], P('lat', 'lon')
Inputs may be any that keep to these rules, and one draw needn't show every extreme that they name: `band_counts`: counts lie between 256 and 512; some band has exactly 512 and some band exactly 256. `halo_rows`: every entry names a live slot of the neighbour band it refers to (the band itself where that neighbour does not exist). `window_mask`: entries are 0 or 1; the middle entry (offset 0) is always 1. `norm_gain`: gains are positive.
All inputs are finite; a program needn't handle non-finite values.
Results may differ from a plain program's by a relative error of at most 0.002.
The roundings to bfloat16 on the way count: a program that leaves them out, or rounds other values in their place, can miss the bound.
Values may be sent and summed in bfloat16 or wider, within the bound.
A program may use at most 192 MiB of HBM per device.

v0:
```python
import functools

import jax
import jax.numpy as jnp
from jax import lax
from jax.experimental import pallas as pl
from jax.experimental.pallas import tpu as pltpu
from jax.sharding import PartitionSpec as P

HEADS = 16
EPS = 1e-05
BIG = 1e30
f32 = jnp.float32
bf16 = jnp.bfloat16
MESH = pl.DeviceIdType.MESH

OWN, PARTNER, NEAR, FAR, SHARED = range(5)


def layer_kernel(
    counts_ref, mask_ref, gain_ref, halo_ref, tokens_ref, wqkv_ref, wout_ref,
    out_ref,
    tok, wq, wo, nown, nrecv, hsend, hrecv, kbuf, vbuf, khalo, vhalo,
    q_ref, m_ref, acc_ref, qb_ref, ones_ref, hones_ref, att, row0,
    in_sem, w_sem, out_sem, send_sem, recv_sem,
):
    lat = lax.axis_index("lat")
    lon = lax.axis_index("lon")
    nlat = lax.axis_size("lat")
    nlon = lax.axis_size("lon")
    rows, width = tok.shape
    chunk = rows // 4
    halo = hsend.shape[1]
    side = 2 * lax.rem(lon, 2) - 1

    def wrap(x):
        return lax.rem(x + nlon, nlon)

    near = (lat, wrap(lon + side))
    far_to = (lat, wrap(lon - 2 * side))
    far_from = (lat, wrap(lon + 2 * side))
    partner = (lat, lon - side)
    south = (lax.rem(lat + 1, nlat), lon)
    north = (lax.rem(lat + nlat - 1, nlat), lon)

    def remote(src, dst, index, device):
        return pltpu.make_async_remote_copy(
            src_ref=src, dst_ref=dst, send_sem=send_sem.at[index], recv_sem=recv_sem.at[index],
            device_id=device, device_id_type=MESH,
        )

    send_near = remote(nown, nrecv.at[0], 0, near)
    send_far = remote(nown, nrecv.at[1], 1, far_to)
    send_south = remote(hsend.at[0], hrecv.at[pl.ds(0, halo)], 2, south)
    send_north = remote(hsend.at[1], hrecv.at[pl.ds(halo, halo)], 3, north)
    send_k = remote(kbuf.at[OWN], kbuf.at[PARTNER], 4, partner)
    send_v = remote(vbuf.at[OWN], vbuf.at[PARTNER], 5, partner)
    share_k = remote(kbuf.at[NEAR], kbuf.at[SHARED], 6, partner)
    share_v = remote(vbuf.at[NEAR], vbuf.at[SHARED], 7, partner)

    barrier = pltpu.get_barrier_semaphore()
    for device in (near, far_to, far_from, partner, south, north):
        pl.semaphore_signal(barrier, inc=1, device_id=device, device_id_type=MESH)

    tok_copies = []
    for r in range(4):
        part = pl.ds(r * chunk, chunk)
        copy = pltpu.make_async_copy(tokens_ref.at[part], tok.at[part], in_sem.at[r])
        copy.start()
        tok_copies.append(copy)
    w_copies = []
    for j in range(3):
        part = pl.ds(j * width, width)
        copy = pltpu.make_async_copy(wqkv_ref.at[:, part], wq.at[:, part], w_sem.at[j])
        copy.start()
        w_copies.append(copy)
    wo_copy = pltpu.make_async_copy(wout_ref, wo, w_sem.at[3])
    wo_copy.start()

    count = counts_ref[0]
    gain = gain_ref[...]

    for r in range(4):
        tok_copies[r].wait()
        x = tok[pl.ds(r * chunk, chunk), :]
        average = jnp.mean(x, axis=-1, keepdims=True)
        centered = x - average
        variance = jnp.mean(centered * centered, axis=-1, keepdims=True)
        y = centered * lax.rsqrt(variance + EPS) * gain
        if r == 0:
            row0[...] = jnp.broadcast_to(y[0:1, :], row0.shape)
        position = r * chunk + lax.broadcasted_iota(jnp.int32, (chunk, 1), 0)
        y = jnp.where(position < count, y, row0[0:1, :])
        nown[pl.ds(r * chunk, chunk), :] = y.astype(bf16)

    to_south = halo_ref[jnp.minimum(lat + 1, nlat - 1), 0:1, :]
    to_north = halo_ref[jnp.maximum(lat - 1, 0), 1:2, :]
    slot = lax.broadcasted_iota(jnp.int32, (rows, halo), 0)
    for j, wanted in ((0, to_south), (1, to_north)):
        pick = jnp.where(slot == wanted, 1.0, 0.0).astype(bf16)
        hsend[j] = lax.dot_general(
            pick, nown[...], (((0,), (0,)), ((), ())), preferred_element_type=f32
        ).astype(bf16)

    pl.semaphore_wait(barrier, 6)
    send_near.start()
    send_south.start()
    send_north.start()
    send_far.start()

    lane = lax.broadcasted_iota(jnp.int32, (1, 128), 1)
    low = lane < 64
    low_f = jnp.where(low, 1.0, 0.0)
    high_f = 1.0 - low_f
    position = lax.broadcasted_iota(jnp.int32, (rows, 1), 0)
    live = position < count
    live_f = jnp.where(live, 1.0, 0.0)
    ones_ref[0] = (live_f * high_f).astype(bf16)
    ones_ref[1] = (live_f * low_f).astype(bf16)
    has_north = jnp.where(lat > 0, 1.0, 0.0)
    has_south = jnp.where(lat < nlat - 1, 1.0, 0.0)
    hrow = lax.broadcasted_iota(jnp.int32, (2 * halo, 1), 0)
    hlive_f = jnp.where(hrow < halo, has_north, has_south)
    hones_ref[0] = (hlive_f * high_f).astype(bf16)
    hones_ref[1] = (hlive_f * low_f).astype(bf16)
    low_b = low_f.astype(bf16)
    high_b = high_f.astype(bf16)

    tile = width // 2

    def project_rows(src, column):
        cols = pl.ds(pl.multiple_of(column, tile), tile)
        return jnp.dot(src[...], wq[:, cols], preferred_element_type=f32)

    def project_k(src, dst):
        for t in range(2):
            dst[:, pl.ds(t * tile, tile)] = project_rows(src, width + t * tile).astype(bf16)

    def project_v(src, dst, alive):
        for t in range(2):
            v = project_rows(src, 2 * width + t * tile)
            dst[:, pl.ds(t * tile, tile)] = jnp.where(alive, v, 0.0).astype(bf16)

    def fill_bias(column):
        for r in range(4):
            seen = mask_ref[r, column].astype(f32)
            qb_ref[pl.ds(r * chunk, chunk), :] = jnp.full((chunk, 128), (1.0 - seen) * BIG, f32)

    def attend(k, v, ones, bias, first=False):
        keys = k.shape[0]
        group = 4

        def body(g, carry):
            for hh in range(group):
                h = g * group + hh
                odd = hh % 2
                cols = pl.ds(pl.multiple_of((g * (group // 2) + hh // 2) * 128, 128), 128)
                s = lax.dot_general(
                    q_ref[h], k[:, cols], (((1,), (1,)), ((), ())), preferred_element_type=f32
                )
                top = jnp.max(s, axis=1, keepdims=True)
                if bias:
                    top = top - qb_ref[...]
                if first:
                    new = jnp.broadcast_to(top, (rows, 128))
                else:
                    old = m_ref[h]
                    new = jnp.maximum(old, top)
                shift = new + qb_ref[...] if bias else new
                p = jnp.exp(s - jnp.tile(shift, (1, keys // 128))).astype(bf16)
                vh = v[:, cols] * (high_b if odd else low_b) + ones[odd]
                o = jnp.dot(p, vh, preferred_element_type=f32)
                if first:
                    acc_ref[h] = o
                else:
                    acc_ref[h] = acc_ref[h] * jnp.exp(old - new) + o
                m_ref[h] = new
            return carry

        lax.fori_loop(0, HEADS // group, body, 0)

    w_copies[0].wait()
    for t in range(2):
        q = project_rows(nown, t * tile) * 0.125
        for j in range(tile // 128):
            pair = q[:, j * 128:(j + 1) * 128]
            h = (t * (tile // 128) + j) * 2
            q_ref[h] = jnp.where(low, pair, 0.0).astype(bf16)
            q_ref[h + 1] = jnp.where(low, 0.0, pair).astype(bf16)
    w_copies[1].wait()
    project_k(nown, kbuf.at[OWN])
    send_k.start()
    w_copies[2].wait()
    project_v(nown, vbuf.at[OWN], live)
    send_v.start()
    attend(kbuf.at[OWN], vbuf.at[OWN], ones_ref, False, first=True)

    send_k.wait_recv()
    send_v.wait_recv()
    fill_bias(2 - side)
    attend(kbuf.at[PARTNER], vbuf.at[PARTNER], ones_ref, True)

    send_south.wait_recv()
    send_north.wait_recv()
    keep = hlive_f > 0.5
    hrecv[...] = jnp.where(keep, hrecv[...].astype(f32), row0[0:1, :]).astype(bf16)
    project_k(hrecv, khalo)
    project_v(hrecv, vhalo, keep)
    attend(khalo, vhalo, hones_ref, False)

    send_near.wait_recv()
    project_k(nrecv.at[0], kbuf.at[NEAR])
    share_k.start()
    project_v(nrecv.at[0], vbuf.at[NEAR], live)
    share_v.start()
    fill_bias(2 + side)
    attend(kbuf.at[NEAR], vbuf.at[NEAR], ones_ref, True)

    send_far.wait_recv()
    project_k(nrecv.at[1], kbuf.at[FAR])
    project_v(nrecv.at[1], vbuf.at[FAR], live)
    fill_bias(2 + 2 * side)
    attend(kbuf.at[FAR], vbuf.at[FAR], ones_ref, True)

    share_k.wait_recv()
    share_v.wait_recv()
    fill_bias(2 - 2 * side)
    attend(kbuf.at[SHARED], vbuf.at[SHARED], ones_ref, True)

    for j in range(HEADS // 2):
        even = acc_ref[2 * j]
        odd = acc_ref[2 * j + 1]
        value = jnp.where(low, even, odd)
        total = pltpu.roll(jnp.where(low, odd, even), 64, axis=1)
        att[:, j * 128:(j + 1) * 128] = (value / total).astype(bf16)
    wo_copy.wait()
    out_copies = []
    for r in range(4):
        part = pl.ds(r * chunk, chunk)
        y = tok[part, :] + jnp.dot(att[part, :], wo[...], preferred_element_type=f32)
        position = r * chunk + lax.broadcasted_iota(jnp.int32, (chunk, 1), 0)
        tok[part, :] = jnp.where(position < count, y, 0.0)
        copy = pltpu.make_async_copy(tok.at[part], out_ref.at[part], out_sem.at[r])
        copy.start()
        out_copies.append(copy)
    for copy in out_copies:
        copy.wait()
    for copy in (send_near, send_far, send_south, send_north, send_k, send_v, share_k, share_v):
        copy.wait_send()


def on_device(tokens, norm_gain, qkv_weight, out_weight, band_counts, halo_rows, window_mask):
    rows, width = tokens.shape[2:]
    halo = halo_rows.shape[2]
    vmem = pl.BlockSpec(memory_space=pltpu.VMEM)
    smem = pl.BlockSpec(memory_space=pltpu.SMEM)
    hbm = pl.BlockSpec(memory_space=pl.ANY)
    dma = pltpu.SemaphoreType.DMA
    out = pl.pallas_call(
        layer_kernel,
        out_shape=jax.ShapeDtypeStruct((rows, width), f32),
        in_specs=[smem, smem, vmem, vmem, hbm, hbm, hbm],
        out_specs=hbm,
        scratch_shapes=[
            pltpu.VMEM((rows, width), f32),
            pltpu.VMEM((width, 3 * width), bf16),
            pltpu.VMEM((width, width), bf16),
            pltpu.VMEM((rows, width), bf16),
            pltpu.VMEM((2, rows, width), bf16),
            pltpu.VMEM((2, halo, width), bf16),
            pltpu.VMEM((2 * halo, width), bf16),
            pltpu.VMEM((5, rows, width), bf16),
            pltpu.VMEM((5, rows, width), bf16),
            pltpu.VMEM((2 * halo, width), bf16),
            pltpu.VMEM((2 * halo, width), bf16),
            pltpu.VMEM((HEADS, rows, 128), bf16),
            pltpu.VMEM((HEADS, rows, 128), f32),
            pltpu.VMEM((HEADS, rows, 128), f32),
            pltpu.VMEM((rows, 128), f32),
            pltpu.VMEM((2, rows, 128), bf16),
            pltpu.VMEM((2, 2 * halo, 128), bf16),
            pltpu.VMEM((rows, width), bf16),
            pltpu.VMEM((8, width), f32),
            dma((4,)),
            dma((4,)),
            dma((4,)),
            dma((8,)),
            dma((8,)),
        ],
        compiler_params=pltpu.CompilerParams(
            collective_id=0, has_side_effects=True, vmem_limit_bytes=66_000_000
        ),
        name="layer",
    )(
        band_counts, window_mask[0, 0], norm_gain[None, :], halo_rows,
        tokens[0, 0], qkv_weight, out_weight,
    )
    return out[None, None]


def solution(mesh):
    in_specs = (
        P("lat", "lon", None, None),
        P(),
        P(),
        P(),
        P("lat"),
        P(),
        P("lat", "lon", None, None),
    )
    out_specs = P("lat", "lon", None, None)
    return jax.shard_map(
        on_device, mesh=mesh, in_specs=in_specs, out_specs=out_specs, check_vma=False
    )
```

profile of v0, /device:TPU:1, one launch (start us, length us, event | category | flops | bytes accessed | tf_op | source)
XLA Modules:
  0.0 81.9 jit_solution(15988505571773626201)
XLA Ops:
  0.7 78.1 %layer.1 = f32[512,1024]{1,0:T(8,128)} custom-call(s32[1]{0:T(128)S(6)} %copy.9.counts_ref, s32[4,5]{1,0:T(4,128)} %bitcast.7, f32[1,1024]{1,0:T(1,128)} %bitcast.6, s32[8,2,128]{2,1,0:T(2,128)} %halo_ref.1, f32[512,1024]{1,0:T(8,128)} %bitcast.5, bf16[1024,3072]{1,0:T(8,128)(2,1)} %wqkv_ref.1, bf16[1024,1024]{1,0:T(8,128)(2,1)} %wout_ref.1), custom_call_target="tpu_custom_call" | custom-call | tf_op jit(solution)/shard_map/layer/pallas_call | solution.py:259
  78.7 3.2 %copy.10 = f32[1,1,512,1024]{3,2,1,0:T(8,128)} copy(f32[1,1,512,1024]{3,2,1,0:T(8,128)} %bitcast.4) | data formatting | bytes 4194304
where the time goes:
time: 82.1 us; the launch traced here: 81.9 us
  Pallas kernels  78.1 us (95%)
  local copies, waits for them, and re-layouts  3.16 us (4%)
    pallas_call x1, Pallas kernels, on_device(): pl.pallas_call(layer_kernel, out_shape=jax.ShapeDtypeStruct((rows, width)...  78.1 us
    unnamed x1, local copies, waits for them, and re-layouts  3.16 us

commit v1 on v0

v1 whole, which is shorter than its diff:
```python
import jax
import jax.numpy as jnp
from jax import lax
from jax.experimental import pallas as pl
from jax.experimental.pallas import tpu as pltpu
from jax.sharding import PartitionSpec as P

HEADS = 16
EPS = 1e-05
BIG = 1e30
LIVE_LANE = 5
f32 = jnp.float32
bf16 = jnp.bfloat16
MESH = pl.DeviceIdType.MESH


def attention_kernel(
    counts_hbm, mask_hbm, gain_hbm, halo_hbm, tokens_ref, wqkv_ref,
    att_ref,
    counts_ref, mask_ref, gain_ref, halo_ref, tok, wq, nown, nrecv, hsend, hrecv, kbuf, vbuf, fk, fq, q_ref, m_ref, acc_ref,
    in_sem, w_sem, small_sem, send_sem, recv_sem,
):
    lat = lax.axis_index("lat")
    lon = lax.axis_index("lon")
    nlat = lax.axis_size("lat")
    nlon = lax.axis_size("lon")
    rows, width = tok.shape
    chunk = rows // 4
    half = rows // 2
    halo = hsend.shape[1]
    side = 2 * lax.rem(lon, 2) - 1

    def wrap(x):
        return lax.rem(x + nlon, nlon)

    partner_row = rows
    near_row = 2 * rows
    halo_row = near_row + rows
    far_row = halo_row + 2 * halo
    shared_row = far_row + rows

    near = (lat, wrap(lon + side))
    far_to = (lat, wrap(lon - 2 * side))
    far_from = (lat, wrap(lon + 2 * side))
    partner = (lat, lon - side)
    south = (lax.rem(lat + 1, nlat), lon)
    north = (lax.rem(lat + nlat - 1, nlat), lon)

    def remote(src, dst, index, device):
        return pltpu.make_async_remote_copy(
            src_ref=src, dst_ref=dst, send_sem=send_sem.at[index], recv_sem=recv_sem.at[index],
            device_id=device, device_id_type=MESH,
        )

    halves = (pl.ds(0, half), pl.ds(half, half))
    send_near = [remote(nown.at[p], nrecv.at[0, p], j, near) for j, p in enumerate(halves)]
    send_far = [remote(nown.at[p], nrecv.at[1, p], 2 + j, far_to) for j, p in enumerate(halves)]
    send_south = remote(hsend.at[0], hrecv.at[pl.ds(0, halo)], 4, south)
    send_north = remote(hsend.at[1], hrecv.at[pl.ds(halo, halo)], 5, north)
    own = pl.ds(0, rows)
    send_k = remote(kbuf.at[own], kbuf.at[pl.ds(partner_row, rows)], 6, partner)
    send_v = remote(vbuf.at[own], vbuf.at[pl.ds(partner_row, rows)], 7, partner)
    here = pl.ds(near_row, rows)
    there = pl.ds(shared_row, rows)
    share_k = remote(kbuf.at[here], kbuf.at[there], 8, partner)
    share_v = remote(vbuf.at[here], vbuf.at[there], 9, partner)

    small_copies = [
        pltpu.make_async_copy(src, dst, small_sem.at[j])
        for j, (src, dst) in enumerate((
            (gain_hbm, gain_ref), (halo_hbm, halo_ref), (counts_hbm, counts_ref),
            (mask_hbm, mask_ref),
        ))
    ]
    small_copies[0].start()
    tok_copies = []
    for r in range(4):
        part = pl.ds(r * chunk, chunk)
        copy = pltpu.make_async_copy(tokens_ref.at[part], tok.at[part], in_sem.at[r])
        copy.start()
        tok_copies.append(copy)
    for copy in small_copies[1:]:
        copy.start()
    w_copies = []
    for j in range(3):
        part = pl.ds(j * width, width)
        w_copies.append(
            pltpu.make_async_copy(wqkv_ref.at[:, part], wq.at[:, part], w_sem.at[j])
        )

    barrier = pltpu.get_barrier_semaphore()
    for device in (near, far_to, far_from, partner, south, north):
        pl.semaphore_signal(barrier, inc=1, device_id=device, device_id_type=MESH)

    small_copies[0].wait()
    gain = gain_ref[...]
    for r in range(4):
        part = pl.ds(r * chunk, chunk)
        tok_copies[r].wait()
        if r > 0:
            w_copies[r - 1].start()
        x = tok[part, :]
        average = jnp.mean(x, axis=-1, keepdims=True)
        centered = x - average
        variance = jnp.mean(centered * centered, axis=-1, keepdims=True)
        nown[part, :] = (centered * lax.rsqrt(variance + EPS) * gain).astype(bf16)
        if r == 1:
            pl.semaphore_wait(barrier, 6)
            send_near[0].start()
    send_near[1].start()
    for copy in small_copies[1:]:
        copy.wait()

    to_south = halo_ref[jnp.minimum(lat + 1, nlat - 1), 0:1, :]
    to_north = halo_ref[jnp.maximum(lat - 1, 0), 1:2, :]
    slot = lax.broadcasted_iota(jnp.int32, (rows, halo), 0)
    for j, wanted in ((0, to_south), (1, to_north)):
        pick = jnp.where(slot == wanted, 1.0, 0.0).astype(bf16)
        hsend[j] = lax.dot_general(
            pick, nown[...], (((0,), (0,)), ((), ())), preferred_element_type=f32
        ).astype(bf16)

    @pl.when(lat == 0)
    def _():
        hrecv[pl.ds(0, halo), :] = jnp.zeros((halo, width), bf16)

    @pl.when(lat == nlat - 1)
    def _():
        hrecv[pl.ds(halo, halo), :] = jnp.zeros((halo, width), bf16)

    count = counts_ref[0]
    lane = lax.broadcasted_iota(jnp.int32, (1, 128), 1)
    low = lane < 64
    for r in range(4):
        feature = jnp.where(lane == LIVE_LANE, 1.0, 0.0)
        for c in range(5):
            hidden = (mask_ref[r, c].astype(f32) - 1.0) * BIG
            feature = feature + jnp.where(lane == c, hidden, 0.0)
        fq[pl.ds(r * chunk, chunk), :] = jnp.broadcast_to(feature, (chunk, 128)).astype(bf16)
    lanes = lax.broadcasted_iota(jnp.int32, (rows, 128), 1)
    position = lax.broadcasted_iota(jnp.int32, (rows, 128), 0)
    dead = jnp.where((lanes == LIVE_LANE) & (position >= count), -BIG, 0.0)
    for row, hops in (
        (0, 0), (partner_row, -side), (near_row, side), (far_row, 2 * side),
        (shared_row, -2 * side),
    ):
        fk[pl.ds(row, rows), :] = jnp.where(lanes == 2 + hops, 1.0, dead).astype(bf16)
    hlanes = lax.broadcasted_iota(jnp.int32, (2 * halo, 128), 1)
    hposition = lax.broadcasted_iota(jnp.int32, (2 * halo, 128), 0)
    gone = jnp.where(
        hposition < halo, jnp.where(lat == 0, -BIG, 0.0), jnp.where(lat == nlat - 1, -BIG, 0.0)
    )
    fk[pl.ds(halo_row, 2 * halo), :] = jnp.where(hlanes == LIVE_LANE, gone, 0.0).astype(bf16)

    low_b = jnp.where(low, 1.0, 0.0).astype(bf16)
    high_b = jnp.where(low, 0.0, 1.0).astype(bf16)

    tile = width // 2

    def project(src, column):
        return jnp.dot(src, wq[:, pl.ds(column, tile)], preferred_element_type=f32)

    def project_to(dst, row, src, column):
        for t in range(2):
            dst[pl.ds(row, src.shape[0]), pl.ds(t * tile, tile)] = project(
                src[...], column + t * tile
            ).astype(bf16)

    def attend(row, keys, first=False, last=False, middle=None):
        group = 4
        part = pl.ds(row, keys)

        def body(g, carry):
            if middle is not None:
                pl.when(g == 1)(middle)
            done = []
            for hh in range(group):
                h = g * group + hh
                odd = hh % 2
                cols = pl.ds(pl.multiple_of((g * (group // 2) + hh // 2) * 128, 128), 128)
                s = lax.dot_general(
                    jnp.concatenate([q_ref[h], fq[...]], axis=1),
                    jnp.concatenate([kbuf[part, cols], fk[part, :]], axis=1),
                    (((1,), (1,)), ((), ())), preferred_element_type=f32,
                )
                new = jnp.max(s, axis=1, keepdims=True)
                if first:
                    new = jnp.broadcast_to(new, (rows, 128))
                else:
                    old = m_ref[h]
                    new = jnp.maximum(old, new)
                p = jnp.exp(s - jnp.tile(new, (1, keys // 128))).astype(bf16)
                mine, other = (high_b, low_b) if odd else (low_b, high_b)
                o = jnp.dot(p, vbuf[part, cols] * mine + other, preferred_element_type=f32)
                if not first:
                    o = acc_ref[h] * jnp.exp(old - new) + o
                if last:
                    done.append(o)
                    if odd:
                        value = jnp.where(low, done[-2], done[-1])
                        total = pltpu.roll(jnp.where(low, done[-1], done[-2]), 64, axis=1)
                        att_ref[:, cols] = (value / total).astype(bf16)
                else:
                    acc_ref[h] = o
                    m_ref[h] = new
            return carry

        lax.fori_loop(0, HEADS // group, body, 0)

    def start_rest():
        pl.when(lat < nlat - 1)(send_south.start)
        pl.when(lat > 0)(send_north.start)
        for copy in send_far:
            copy.start()

    w_copies[0].wait()
    for t in range(2):
        q = project(nown[...], t * tile) * 0.125
        for j in range(tile // 128):
            pair = q[:, j * 128:(j + 1) * 128]
            h = (t * (tile // 128) + j) * 2
            q_ref[h] = jnp.where(low, pair, 0.0).astype(bf16)
            q_ref[h + 1] = jnp.where(low, 0.0, pair).astype(bf16)
    w_copies[1].wait()
    project_to(kbuf, 0, nown, width)
    send_k.start()
    w_copies[2].wait()
    project_to(vbuf, 0, nown, 2 * width)
    send_v.start()

    send_k.wait_recv()
    send_v.wait_recv()
    attend(0, 2 * rows, first=True, middle=start_rest)

    for copy in send_near:
        copy.wait_recv()
    project_to(kbuf, near_row, nrecv.at[0], width)
    share_k.start()
    project_to(vbuf, near_row, nrecv.at[0], 2 * width)
    share_v.start()
    attend(near_row, rows)

    pl.when(lat > 0)(send_south.wait_recv)
    pl.when(lat < nlat - 1)(send_north.wait_recv)
    project_to(kbuf, halo_row, hrecv, width)
    project_to(vbuf, halo_row, hrecv, 2 * width)
    for j, p in enumerate(halves):
        send_far[j].wait_recv()
        row = far_row + j * half
        project_to(kbuf, row, nrecv.at[1, p], width)
        project_to(vbuf, row, nrecv.at[1, p], 2 * width)
    share_k.wait_recv()
    share_v.wait_recv()
    attend(halo_row, 2 * halo + 2 * rows, last=True)

    for copy in (*send_near, *send_far, send_k, send_v, share_k, share_v):
        copy.wait_send()

    pl.when(lat < nlat - 1)(send_south.wait_send)
    pl.when(lat > 0)(send_north.wait_send)


def output_kernel(counts_ref, att_ref, tokens_ref, wout_ref, out_ref):
    chunk = out_ref.shape[0]
    y = tokens_ref[...] + jnp.dot(att_ref[...], wout_ref[...], preferred_element_type=f32)
    position = pl.program_id(0) * chunk + lax.broadcasted_iota(jnp.int32, (chunk, 1), 0)
    out_ref[...] = jnp.where(position < counts_ref[0], y, 0.0)


def on_device(tokens, norm_gain, qkv_weight, out_weight, band_counts, halo_rows, window_mask):
    rows, width = tokens.shape[2:]
    halo = halo_rows.shape[2]
    vmem = pl.BlockSpec(memory_space=pltpu.VMEM)
    smem = pl.BlockSpec(memory_space=pltpu.SMEM)
    hbm = pl.BlockSpec(memory_space=pltpu.MemorySpace.HBM)
    dma = pltpu.SemaphoreType.DMA
    keys = 5 * rows + 2 * halo
    att = pl.pallas_call(
        attention_kernel,
        out_shape=jax.ShapeDtypeStruct((rows, width), bf16),
        in_specs=[hbm] * 6,
        out_specs=vmem,
        scratch_shapes=[
            pltpu.SMEM(band_counts.shape, jnp.int32),
            pltpu.SMEM(window_mask.shape[2:], jnp.int32),
            pltpu.VMEM((1, width), f32),
            pltpu.VMEM(halo_rows.shape, jnp.int32),
            pltpu.VMEM((rows, width), f32),
            pltpu.VMEM((width, 3 * width), bf16),
            pltpu.VMEM((rows, width), bf16),
            pltpu.VMEM((2, rows, width), bf16),
            pltpu.VMEM((2, halo, width), bf16),
            pltpu.VMEM((2 * halo, width), bf16),
            pltpu.VMEM((keys, width), bf16),
            pltpu.VMEM((keys, width), bf16),
            pltpu.VMEM((keys, 128), bf16),
            pltpu.VMEM((rows, 128), bf16),
            pltpu.VMEM((HEADS, rows, 128), bf16),
            pltpu.VMEM((HEADS, rows, 128), f32),
            pltpu.VMEM((HEADS, rows, 128), f32),
            dma((4,)),
            dma((3,)),
            dma((4,)),
            dma((10,)),
            dma((10,)),
        ],
        compiler_params=pltpu.CompilerParams(
            collective_id=0, has_side_effects=True, vmem_limit_bytes=56_000_000
        ),
        name="attention",
    )(
        band_counts, window_mask[0, 0], norm_gain[None, :], halo_rows,
        tokens[0, 0], qkv_weight,
    )
    chunk = rows // 4
    out = pl.pallas_call(
        output_kernel,
        out_shape=jax.ShapeDtypeStruct((rows, width), f32),
        grid=(4,),
        in_specs=[
            smem,
            pl.BlockSpec((chunk, width), lambda i: (i, 0)),
            pl.BlockSpec((chunk, width), lambda i: (i, 0)),
            vmem,
        ],
        out_specs=pl.BlockSpec((chunk, width), lambda i: (i, 0)),
        compiler_params=pltpu.CompilerParams(vmem_limit_bytes=20_000_000),
        name="output",
    )(band_counts, att, tokens[0, 0], out_weight)
    return out[None, None]


def solution(mesh):
    in_specs = (
        P("lat", "lon", None, None),
        P(),
        P(),
        P(),
        P("lat"),
        P(),
        P("lat", "lon", None, None),
    )
    out_specs = P("lat", "lon", None, None)
    return jax.shard_map(
        on_device, mesh=mesh, in_specs=in_specs, out_specs=out_specs, check_vma=False
    )
```

time: 82.1 us -> 71.1 us (0.87)
  Pallas kernels: 78.1 us -> 66.9 us
    pallas_call x1 -> x2, Pallas kernels: 78.1 us -> 66.9 us  [the longest x1 63.9 us: on_device(): pl.pallas_call(attention_kernel, out_shape=jax.ShapeDtypeStruct((rows, wi...]
    unnamed x1 -> x12, local copies, waits for them, and re-layouts: 3.16 us -> 3.28 us
where the time goes in v1:
time: 71.1 us; the launch traced here: 70.9 us
  Pallas kernels  66.9 us (94%)
  local copies, waits for them, and re-layouts  3.28 us (5%)
    pallas_call x1, Pallas kernels, on_device(): pl.pallas_call(attention_kernel, out_shape=jax.ShapeDtypeStruct((rows, wi...  63.9 us
    unnamed x12, local copies, waits for them, and re-layouts  3.28 us
    pallas_call x1, Pallas kernels, on_device(): pl.pallas_call(output_kernel, out_shape=jax.ShapeDtypeStruct((rows, width...  3 us

profile of v1, /device:TPU:1, one launch (start us, length us, event | category | flops | bytes accessed | tf_op | source)
XLA Modules:
  0.0 70.9 jit_solution(13325333337740250118)
XLA Ops:
  0.7 0.0 copy-start.3
  0.7 0.7 copy-done.3
  1.4 0.0 copy-start.4
  1.4 0.7 copy-done.4
  2.0 0.0 copy-start.5
  2.0 0.7 copy-done.5
  2.7 0.0 copy-start
  2.7 0.0 copy-start.2
  2.7 63.9 %attention.1.att_ref = bf16[512,1024]{1,0:T(8,128)(2,1)} custom-call(s32[1]{0:T(128)S(6)} %copy.8.counts_hbm.counts_ref, s32[4,5]{1,0:T(4,128)S(1)} %bitcast.7, f32[1,1024]{1,0:T(1,128)S(1)} %bitcast.6, s32[8,2,128]{2,1,0:T(2,128)S(1)} %copy-done.3, f32[512,1024]{1,0:T(8,128)} %bitcast.4, bf16[1024,3072]{1,0:T(8,128)(2,1)} %wqkv_ref.1), custom_call_target="tpu_custom_call" | custom-call | tf_op jit(solution)/shard_map/attention/pallas_call | solution.py:278
  66.6 0.0 copy-done
  66.6 0.0 copy-done.2
  66.6 0.0 copy-start.1
  66.6 1.2 %copy-done.1 = bf16[512,1024]{1,0:T(8,128)(2,1)S(1)} copy-done((bf16[512,1024]{1,0:T(8,128)(2,1)S(1)}, bf16[512,1024]{1,0:T(8,128)(2,1)}, u32[]{:S(2)}) %copy-start.1) | copy-done | bytes 1048600
  67.9 3.0 %output.1 = f32[512,1024]{1,0:T(8,128)} custom-call(s32[1]{0:T(128)S(6)} %copy.8.counts_hbm.counts_ref, bf16[512,1024]{1,0:T(8,128)(2,1)S(1)} %copy-done.1, f32[512,1024]{1,0:T(8,128)S(1)} %bitcast.5, bf16[1024,1024]{1,0:T(8,128)(2,1)S(1)} %copy-done.2), custom_call_target="tpu_custom_call" | custom-call | tf_op jit(solution)/shard_map/output/pallas_call | solution.py:316
Async XLA Ops:
  0.7 0.7 copy-start.3
  1.4 0.7 copy-start.4
  2.0 0.7 copy-start.5
  2.7 63.9 %copy-start = (f32[1,1,512,1024]{3,2,1,0:T(8,128)S(1)}, f32[1,1,512,1024]{3,2,1,0:T(8,128)}, u32[]{:S(2)}) copy-start(f32[1,1,512,1024]{3,2,1,0:T(8,128)} %param.7) | copy-start | bytes 6291460
  2.7 63.9 %copy-start.2 = (bf16[1024,1024]{1,0:T(8,128)(2,1)S(1)}, bf16[1024,1024]{1,0:T(8,128)(2,1)}, u32[]{:S(2)}) copy-start(bf16[1024,1024]{1,0:T(8,128)(2,1)} %wout_ref.1) | copy-start | bytes 6291460
  66.6 1.2 %copy-start.1 = (bf16[512,1024]{1,0:T(8,128)(2,1)S(1)}, bf16[512,1024]{1,0:T(8,128)(2,1)}, u32[]{:S(2)}) copy-start(bf16[512,1024]{1,0:T(8,128)(2,1)} %attention.1.att_ref) | copy-start | bytes 3145732

commit v2 on v1

--- a/solution.py
+++ b/solution.py
@@ -17,8 +17,8 @@
 def attention_kernel(
     counts_hbm, mask_hbm, gain_hbm, halo_hbm, tokens_ref, wqkv_ref,
     att_ref,
-    counts_ref, mask_ref, gain_ref, halo_ref, tok, wq, nown, nrecv, hsend, hrecv, kbuf, vbuf, fk, fq, q_ref, m_ref, acc_ref,
-    in_sem, w_sem, small_sem, send_sem, recv_sem,
+    counts_ref, mask_ref, gain_ref, halo_ref, tok, wq, nown, nrecv, hsend, hrecv, kbuf, vbuf, fk, fq, q_ref, m_ref, acc_ref, att,
+    in_sem, w_sem, small_sem, att_sem, send_sem, recv_sem,
 ):
     lat = lax.axis_index("lat")
     lon = lax.axis_index("lon")
@@ -35,9 +35,9 @@
 
     partner_row = rows
     near_row = 2 * rows
-    halo_row = near_row + rows
+    shared_row = near_row + rows
+    halo_row = shared_row + rows
     far_row = halo_row + 2 * halo
-    shared_row = far_row + rows
 
     near = (lat, wrap(lon + side))
     far_to = (lat, wrap(lon - 2 * side))
@@ -89,8 +89,22 @@
         )
 
     barrier = pltpu.get_barrier_semaphore()
-    for device in (near, far_to, far_from, partner, south, north):
+
+    def greet(device):
         pl.semaphore_signal(barrier, inc=1, device_id=device, device_id_type=MESH)
+
+    for device in (near, far_to, far_from, partner):
+        greet(device)
+
+    @pl.when(lat < nlat - 1)
+    def _():
+        greet(south)
+
+    @pl.when(lat > 0)
+    def _():
+        greet(north)
+
+    greeted = 4 + jnp.where(lat < nlat - 1, 1, 0) + jnp.where(lat > 0, 1, 0)
 
     small_copies[0].wait()
     gain = gain_ref[...]
@@ -105,7 +119,7 @@
         variance = jnp.mean(centered * centered, axis=-1, keepdims=True)
         nown[part, :] = (centered * lax.rsqrt(variance + EPS) * gain).astype(bf16)
         if r == 1:
-            pl.semaphore_wait(barrier, 6)
+            pl.semaphore_wait(barrier, greeted)
             send_near[0].start()
     send_near[1].start()
     for copy in small_copies[1:]:
@@ -166,13 +180,17 @@
                 src[...], column + t * tile
             ).astype(bf16)
 
-    def attend(row, keys, first=False, last=False, middle=None):
+    def att_copy(g):
+        cols = pl.ds(pl.multiple_of(g * 256, 256), 256)
+        return pltpu.make_async_copy(att.at[g], att_ref.at[:, cols], att_sem.at[g])
+
+    def attend(row, keys, first=False, last=False, between=()):
         group = 4
         part = pl.ds(row, keys)
 
         def body(g, carry):
-            if middle is not None:
-                pl.when(g == 1)(middle)
+            for n, action in enumerate(between):
+                pl.when(g == n + 1)(action)
             done = []
             for hh in range(group):
                 h = g * group + hh
@@ -199,10 +217,12 @@
                     if odd:
                         value = jnp.where(low, done[-2], done[-1])
                         total = pltpu.roll(jnp.where(low, done[-1], done[-2]), 64, axis=1)
-                        att_ref[:, cols] = (value / total).astype(bf16)
+                        att[g, :, (hh // 2) * 128:(hh // 2 + 1) * 128] = (value / total).astype(bf16)
                 else:
                     acc_ref[h] = o
                     m_ref[h] = new
+            if last:
+                att_copy(g).start()
             return carry
 
         lax.fori_loop(0, HEADS // group, body, 0)
@@ -212,6 +232,14 @@
         pl.when(lat > 0)(send_north.start)
         for copy in send_far:
             copy.start()
+
+    def share_near():
+        for copy in send_near:
+            copy.wait_recv()
+        project_to(kbuf, near_row, nrecv.at[0], width)
+        share_k.start()
+        project_to(vbuf, near_row, nrecv.at[0], 2 * width)
+        share_v.start()
 
     w_copies[0].wait()
     for t in range(2):
@@ -230,15 +258,11 @@
 
     send_k.wait_recv()
     send_v.wait_recv()
-    attend(0, 2 * rows, first=True, middle=start_rest)
-
-    for copy in send_near:
-        copy.wait_recv()
-    project_to(kbuf, near_row, nrecv.at[0], width)
-    share_k.start()
-    project_to(vbuf, near_row, nrecv.at[0], 2 * width)
-    share_v.start()
-    attend(near_row, rows)
+    attend(0, 2 * rows, first=True, between=(start_rest, share_near))
+
+    share_k.wait_recv()
+    share_v.wait_recv()
+    attend(near_row, 2 * rows)
 
     pl.when(lat > 0)(send_south.wait_recv)
     pl.when(lat < nlat - 1)(send_north.wait_recv)
@@ -249,9 +273,9 @@
         row = far_row + j * half
         project_to(kbuf, row, nrecv.at[1, p], width)
         project_to(vbuf, row, nrecv.at[1, p], 2 * width)
-    share_k.wait_recv()
-    share_v.wait_recv()
-    attend(halo_row, 2 * halo + 2 * rows, last=True)
+    attend(halo_row, 2 * halo + rows, last=True)
+    for g in range(HEADS // 4):
+        att_copy(g).wait()
 
     for copy in (*send_near, *send_far, send_k, send_v, share_k, share_v):
         copy.wait_send()
@@ -260,17 +284,38 @@
     pl.when(lat > 0)(send_north.wait_send)
 
 
-def output_kernel(counts_ref, att_ref, tokens_ref, wout_ref, out_ref):
-    chunk = out_ref.shape[0]
-    y = tokens_ref[...] + jnp.dot(att_ref[...], wout_ref[...], preferred_element_type=f32)
-    position = pl.program_id(0) * chunk + lax.broadcasted_iota(jnp.int32, (chunk, 1), 0)
-    out_ref[...] = jnp.where(position < counts_ref[0], y, 0.0)
+def output_kernel(
+    counts_ref, att_hbm, tokens_hbm, wout_hbm, out_hbm, att, tok, wo, out, in_sem, w_sem, out_sem
+):
+    rows, width = tok.shape
+    tiles = w_sem.shape[0]
+    parts = [pl.ds(j * (width // tiles), width // tiles) for j in range(tiles)]
+    att_copy = pltpu.make_async_copy(att_hbm, att, in_sem.at[tiles])
+    att_copy.start()
+    w_copies = []
+    tok_copies = []
+    for j, p in enumerate(parts):
+        w_copies.append(pltpu.make_async_copy(wout_hbm.at[:, p], wo.at[:, p], w_sem.at[j]))
+        w_copies[j].start()
+        tok_copies.append(pltpu.make_async_copy(tokens_hbm.at[:, p], tok.at[:, p], in_sem.at[j]))
+        tok_copies[j].start()
+    live = lax.broadcasted_iota(jnp.int32, (rows, 1), 0) < counts_ref[0]
+    att_copy.wait()
+    out_copies = []
+    for j, p in enumerate(parts):
+        w_copies[j].wait()
+        tok_copies[j].wait()
+        y = tok[:, p] + jnp.dot(att[...], wo[:, p], preferred_element_type=f32)
+        out[:, p] = jnp.where(live, y, 0.0)
+        out_copies.append(pltpu.make_async_copy(out.at[:, p], out_hbm.at[:, p], out_sem.at[j]))
+        out_copies[j].start()
+    for copy in out_copies:
+        copy.wait()
 
 
 def on_device(tokens, norm_gain, qkv_weight, out_weight, band_counts, halo_rows, window_mask):
     rows, width = tokens.shape[2:]
     halo = halo_rows.shape[2]
-    vmem = pl.BlockSpec(memory_space=pltpu.VMEM)
     smem = pl.BlockSpec(memory_space=pltpu.SMEM)
     hbm = pl.BlockSpec(memory_space=pltpu.MemorySpace.HBM)
     dma = pltpu.SemaphoreType.DMA
@@ -279,7 +324,7 @@
         attention_kernel,
         out_shape=jax.ShapeDtypeStruct((rows, width), bf16),
         in_specs=[hbm] * 6,
-        out_specs=vmem,
+        out_specs=hbm,
         scratch_shapes=[
             pltpu.SMEM(band_counts.shape, jnp.int32),
             pltpu.SMEM(window_mask.shape[2:], jnp.int32),
@@ -298,33 +343,37 @@
             pltpu.VMEM((HEADS, rows, 128), bf16),
             pltpu.VMEM((HEADS, rows, 128), f32),
             pltpu.VMEM((HEADS, rows, 128), f32),
+            pltpu.VMEM((HEADS // 4, rows, 256), bf16),
             dma((4,)),
             dma((3,)),
             dma((4,)),
+            dma((HEADS // 4,)),
             dma((10,)),
             dma((10,)),
         ],
         compiler_params=pltpu.CompilerParams(
-            collective_id=0, has_side_effects=True, vmem_limit_bytes=56_000_000
+            collective_id=0, has_side_effects=True, vmem_limit_bytes=67_000_000
         ),
         name="attention",
     )(
         band_counts, window_mask[0, 0], norm_gain[None, :], halo_rows,
         tokens[0, 0], qkv_weight,
     )
-    chunk = rows // 4
     out = pl.pallas_call(
         output_kernel,
         out_shape=jax.ShapeDtypeStruct((rows, width), f32),
-        grid=(4,),
-        in_specs=[
-            smem,
-            pl.BlockSpec((chunk, width), lambda i: (i, 0)),
-            pl.BlockSpec((chunk, width), lambda i: (i, 0)),
-            vmem,
+        in_specs=[smem, hbm, hbm, hbm],
+        out_specs=hbm,
+        scratch_shapes=[
+            pltpu.VMEM((rows, width), bf16),
+            pltpu.VMEM((rows, width), f32),
+            pltpu.VMEM((width, width), bf16),
+            pltpu.VMEM((rows, width), f32),
+            dma((5,)),
+            dma((4,)),
+            dma((4,)),
         ],
-        out_specs=pl.BlockSpec((chunk, width), lambda i: (i, 0)),
-        compiler_params=pltpu.CompilerParams(vmem_limit_bytes=20_000_000),
+        compiler_params=pltpu.CompilerParams(vmem_limit_bytes=67_000_000),
         name="output",
     )(band_counts, att, tokens[0, 0], out_weight)
     return out[None, None]

time: 71.1 us -> 65 us (0.914)
  local copies, waits for them, and re-layouts: 3.28 us -> 0 us
  Pallas kernels: 66.9 us -> 64 us
    pallas_call x1, Pallas kernels: 63.9 us -> 58.8 us  [on_device(): pl.pallas_call(attention_kernel, out_shape=jax.ShapeDtypeStruct((rows, wi...]
    unnamed x12 -> x0, local copies, waits for them, and re-layouts: 3.28 us -> none
    pallas_call x1, Pallas kernels: 3 us -> 5.21 us  [on_device(): pl.pallas_call(output_kernel, out_shape=jax.ShapeDtypeStruct((rows, width...]
where the time goes in v2:
time: 65 us; the launch traced here: 64.8 us
  Pallas kernels  64 us (98%)
  between operations  0.84 us (1%)
    pallas_call x1, Pallas kernels, on_device(): pl.pallas_call(attention_kernel, out_shape=jax.ShapeDtypeStruct((rows, wi...  58.8 us
    pallas_call x1, Pallas kernels, on_device(): pl.pallas_call(output_kernel, out_shape=jax.ShapeDtypeStruct((rows, width...  5.21 us

profile of v2, /device:TPU:1, one launch (start us, length us, event | category | flops | bytes accessed | tf_op | source)
XLA Modules:
  0.0 64.8 jit_solution(5895371491480786051)
XLA Ops:
  0.7 58.8 %attention.1.att_hbm = bf16[512,1024]{1,0:T(8,128)(2,1)} custom-call(s32[1]{0:T(128)S(6)} %copy.8.counts_hbm.counts_ref, s32[4,5]{1,0:T(4,128)} %bitcast.7, f32[1,1024]{1,0:T(1,128)} %bitcast.6, s32[8,2,128]{2,1,0:T(2,128)} %halo_hbm.1, f32[512,1024]{1,0:T(8,128)} %bitcast.4, bf16[1024,3072]{1,0:T(8,128)(2,1)} %wqkv_ref.1), custom_call_target="tpu_custom_call" | custom-call | tf_op jit(solution)/shard_map/attention/pallas_call | solution.py:323
  59.4 5.2 %output.1 = f32[512,1024]{1,0:T(8,128)} custom-call(s32[1]{0:T(128)S(6)} %copy.8.counts_hbm.counts_ref, bf16[512,1024]{1,0:T(8,128)(2,1)} %attention.1.att_hbm, f32[512,1024]{1,0:T(8,128)} %bitcast.5, bf16[1024,1024]{1,0:T(8,128)(2,1)} %wout_hbm.1), custom_call_target="tpu_custom_call" | custom-call | tf_op jit(solution)/shard_map/output/pallas_call | solution.py:362

commit v3 on v2

--- a/solution.py
+++ b/solution.py
@@ -17,7 +17,7 @@
 def attention_kernel(
     counts_hbm, mask_hbm, gain_hbm, halo_hbm, tokens_ref, wqkv_ref,
     att_ref,
-    counts_ref, mask_ref, gain_ref, halo_ref, tok, wq, nown, nrecv, hsend, hrecv, kbuf, vbuf, fk, fq, q_ref, m_ref, acc_ref, att,
+    counts_ref, mask_ref, gain_ref, halo_ref, tok, wq, nown, nrecv, hsend, hrecv, kbuf, vbuf, fk, fq, q_ref, m_ref, acc_ref, att, sbuf,
     in_sem, w_sem, small_sem, att_sem, send_sem, recv_sem,
 ):
     lat = lax.axis_index("lat")
@@ -187,6 +187,20 @@
     def attend(row, keys, first=False, last=False, between=()):
         group = 4
         part = pl.ds(row, keys)
+        steps = HEADS // group
+
+        def columns(g, hh):
+            return pl.ds(pl.multiple_of((g * (group // 2) + hh // 2) * 128, 128), 128)
+
+        def scores(g, hh):
+            return lax.dot_general(
+                jnp.concatenate([q_ref[g * group + hh], fq[...]], axis=1),
+                jnp.concatenate([kbuf[part, columns(g, hh)], fk[part, :]], axis=1),
+                (((1,), (1,)), ((), ())), preferred_element_type=f32,
+            )
+
+        held = pl.ds(0, keys)
+        sbuf[0, :, held] = scores(0, 0)
 
         def body(g, carry):
             for n, action in enumerate(between):
@@ -195,12 +209,12 @@
             for hh in range(group):
                 h = g * group + hh
                 odd = hh % 2
-                cols = pl.ds(pl.multiple_of((g * (group // 2) + hh // 2) * 128, 128), 128)
-                s = lax.dot_general(
-                    jnp.concatenate([q_ref[h], fq[...]], axis=1),
-                    jnp.concatenate([kbuf[part, cols], fk[part, :]], axis=1),
-                    (((1,), (1,)), ((), ())), preferred_element_type=f32,
-                )
+                cols = columns(g, hh)
+                if hh + 1 < group:
+                    later = scores(g, hh + 1)
+                else:
+                    later = scores(jnp.minimum(g + 1, steps - 1), 0)
+                s = sbuf[odd, :, held]
                 new = jnp.max(s, axis=1, keepdims=True)
                 if first:
                     new = jnp.broadcast_to(new, (rows, 128))
@@ -221,11 +235,12 @@
                 else:
                     acc_ref[h] = o
                     m_ref[h] = new
+                sbuf[1 - odd, :, held] = later
             if last:
                 att_copy(g).start()
             return carry
 
-        lax.fori_loop(0, HEADS // group, body, 0)
+        lax.fori_loop(0, steps, body, 0)
 
     def start_rest():
         pl.when(lat < nlat - 1)(send_south.start)
@@ -344,6 +359,7 @@
             pltpu.VMEM((HEADS, rows, 128), f32),
             pltpu.VMEM((HEADS, rows, 128), f32),
             pltpu.VMEM((HEADS // 4, rows, 256), bf16),
+            pltpu.VMEM((2, rows, 2 * rows), f32),
             dma((4,)),
             dma((3,)),
             dma((4,)),
@@ -369,9 +385,9 @@
             pltpu.VMEM((rows, width), f32),
             pltpu.VMEM((width, width), bf16),
             pltpu.VMEM((rows, width), f32),
-            dma((5,)),
-            dma((4,)),
-            dma((4,)),
+            dma((3,)),
+            dma((2,)),
+            dma((2,)),
         ],
         compiler_params=pltpu.CompilerParams(vmem_limit_bytes=67_000_000),
         name="output",

time: 65 us -> 62.6 us (0.963)
  Pallas kernels: 64 us -> 61.6 us
    pallas_call x1, Pallas kernels: 58.8 us -> 57.3 us  [on_device(): pl.pallas_call(attention_kernel, out_shape=jax.ShapeDtypeStruct((rows, wi...]
    pallas_call x1, Pallas kernels: 5.21 us -> 4.3 us  [on_device(): pl.pallas_call(output_kernel, out_shape=jax.ShapeDtypeStruct((rows, width...]
where the time goes in v3:
time: 62.6 us; the launch traced here: 62.4 us
  Pallas kernels  61.6 us (98%)
  between operations  0.84 us (1%)
    pallas_call x1, Pallas kernels, on_device(): pl.pallas_call(attention_kernel, out_shape=jax.ShapeDtypeStruct((rows, wi...  57.3 us
    pallas_call x1, Pallas kernels, on_device(): pl.pallas_call(output_kernel, out_shape=jax.ShapeDtypeStruct((rows, width...  4.3 us

profile of v3, /device:TPU:1, one launch (start us, length us, event | category | flops | bytes accessed | tf_op | source)
XLA Modules:
  0.0 62.4 jit_solution(11467099503191578242)
XLA Ops:
  0.7 57.3 %attention.1.att_hbm = bf16[512,1024]{1,0:T(8,128)(2,1)} custom-call(s32[1]{0:T(128)S(6)} %copy.8.counts_hbm.counts_ref, s32[4,5]{1,0:T(4,128)} %bitcast.7, f32[1,1024]{1,0:T(1,128)} %bitcast.6, s32[8,2,128]{2,1,0:T(2,128)} %halo_hbm.1, f32[512,1024]{1,0:T(8,128)} %bitcast.4, bf16[1024,3072]{1,0:T(8,128)(2,1)} %wqkv_ref.1), custom_call_target="tpu_custom_call" | custom-call | tf_op jit(solution)/shard_map/attention/pallas_call | solution.py:338
  57.9 4.3 %output.1 = f32[512,1024]{1,0:T(8,128)} custom-call(s32[1]{0:T(128)S(6)} %copy.8.counts_hbm.counts_ref, bf16[512,1024]{1,0:T(8,128)(2,1)} %attention.1.att_hbm, f32[512,1024]{1,0:T(8,128)} %bitcast.5, bf16[1024,1024]{1,0:T(8,128)(2,1)} %wout_hbm.1), custom_call_target="tpu_custom_call" | custom-call | tf_op jit(solution)/shard_map/output/pallas_call | solution.py:378

commit v4 on v3

--- a/solution.py
+++ b/solution.py
@@ -242,9 +242,7 @@
 
         lax.fori_loop(0, steps, body, 0)
 
-    def start_rest():
-        pl.when(lat < nlat - 1)(send_south.start)
-        pl.when(lat > 0)(send_north.start)
+    def start_far():
         for copy in send_far:
             copy.start()
 
@@ -273,22 +271,26 @@
 
     send_k.wait_recv()
     send_v.wait_recv()
-    attend(0, 2 * rows, first=True, between=(start_rest, share_near))
+    attend(0, 2 * rows, first=True, between=(start_far, share_near))
+    pl.when(lat < nlat - 1)(send_south.start)
+    pl.when(lat > 0)(send_north.start)
 
     share_k.wait_recv()
     share_v.wait_recv()
     attend(near_row, 2 * rows)
 
-    pl.when(lat > 0)(send_south.wait_recv)
-    pl.when(lat < nlat - 1)(send_north.wait_recv)
-    project_to(kbuf, halo_row, hrecv, width)
-    project_to(vbuf, halo_row, hrecv, 2 * width)
     for j, p in enumerate(halves):
         send_far[j].wait_recv()
         row = far_row + j * half
         project_to(kbuf, row, nrecv.at[1, p], width)
         project_to(vbuf, row, nrecv.at[1, p], 2 * width)
-    attend(halo_row, 2 * halo + rows, last=True)
+    attend(far_row, rows)
+
+    pl.when(lat > 0)(send_south.wait_recv)
+    pl.when(lat < nlat - 1)(send_north.wait_recv)
+    project_to(kbuf, halo_row, hrecv, width)
+    project_to(vbuf, halo_row, hrecv, 2 * width)
+    attend(halo_row, 2 * halo, last=True)
     for g in range(HEADS // 4):
         att_copy(g).wait()
 

time: 62.6 us -> 60.4 us (0.965)
  Pallas kernels: 61.6 us -> 59.5 us
    pallas_call x1, Pallas kernels: 57.3 us -> 55.2 us  [on_device(): pl.pallas_call(attention_kernel, out_shape=jax.ShapeDtypeStruct((rows, wi...]
where the time goes in v4:
time: 60.4 us; the launch traced here: 60.3 us
  Pallas kernels  59.5 us (99%)
  between operations  0.82 us (1%)
    pallas_call x1, Pallas kernels, on_device(): pl.pallas_call(attention_kernel, out_shape=jax.ShapeDtypeStruct((rows, wi...  55.2 us
    pallas_call x1, Pallas kernels, on_device(): pl.pallas_call(output_kernel, out_shape=jax.ShapeDtypeStruct((rows, width...  4.3 us

profile of v4, /device:TPU:1, one launch (start us, length us, event | category | flops | bytes accessed | tf_op | source)
XLA Modules:
  0.0 60.3 jit_solution(2340043338397954083)
XLA Ops:
  0.7 55.2 %attention.1.att_hbm = bf16[512,1024]{1,0:T(8,128)(2,1)} custom-call(s32[1]{0:T(128)S(6)} %copy.8.counts_hbm.counts_ref, s32[4,5]{1,0:T(4,128)} %bitcast.7, f32[1,1024]{1,0:T(1,128)} %bitcast.6, s32[8,2,128]{2,1,0:T(2,128)} %halo_hbm.1, f32[512,1024]{1,0:T(8,128)} %bitcast.4, bf16[1024,3072]{1,0:T(8,128)(2,1)} %wqkv_ref.1), custom_call_target="tpu_custom_call" | custom-call | tf_op jit(solution)/shard_map/attention/pallas_call | solution.py:340
  55.8 4.3 %output.1 = f32[512,1024]{1,0:T(8,128)} custom-call(s32[1]{0:T(128)S(6)} %copy.8.counts_hbm.counts_ref, bf16[512,1024]{1,0:T(8,128)(2,1)} %attention.1.att_hbm, f32[512,1024]{1,0:T(8,128)} %bitcast.5, bf16[1024,1024]{1,0:T(8,128)(2,1)} %wout_hbm.1), custom_call_target="tpu_custom_call" | custom-call | tf_op jit(solution)/shard_map/output/pallas_call | solution.py:380

commit v5 on v4

--- a/solution.py
+++ b/solution.py
@@ -184,8 +184,7 @@
         cols = pl.ds(pl.multiple_of(g * 256, 256), 256)
         return pltpu.make_async_copy(att.at[g], att_ref.at[:, cols], att_sem.at[g])
 
-    def attend(row, keys, first=False, last=False, between=()):
-        group = 4
+    def attend(row, keys, first=False, last=False, between=(), group=4):
         part = pl.ds(row, keys)
         steps = HEADS // group
 
@@ -277,14 +276,14 @@
 
     share_k.wait_recv()
     share_v.wait_recv()
-    attend(near_row, 2 * rows)
+    attend(near_row, 2 * rows, group=8)
 
     for j, p in enumerate(halves):
         send_far[j].wait_recv()
         row = far_row + j * half
         project_to(kbuf, row, nrecv.at[1, p], width)
         project_to(vbuf, row, nrecv.at[1, p], 2 * width)
-    attend(far_row, rows)
+    attend(far_row, rows, group=8)
 
     pl.when(lat > 0)(send_south.wait_recv)
     pl.when(lat < nlat - 1)(send_north.wait_recv)

time: 60.4 us -> 59.9 us (level)
  no operation moved by 1% of the time
where the time goes in v5:
time: 59.9 us; the launch traced here: 59.7 us
  Pallas kernels  58.9 us (98%)
  between operations  0.84 us (1%)
    pallas_call x1, Pallas kernels, on_device(): pl.pallas_call(attention_kernel, out_shape=jax.ShapeDtypeStruct((rows, wi...  54.6 us
    pallas_call x1, Pallas kernels, on_device(): pl.pallas_call(output_kernel, out_shape=jax.ShapeDtypeStruct((rows, width...  4.3 us

profile of v5, /device:TPU:1, one launch (start us, length us, event | category | flops | bytes accessed | tf_op | source)
XLA Modules:
  0.0 59.7 jit_solution(16020096361359530287)
XLA Ops:
  0.7 54.6 %attention.1.att_hbm = bf16[512,1024]{1,0:T(8,128)(2,1)} custom-call(s32[1]{0:T(128)S(6)} %copy.8.counts_hbm.counts_ref, s32[4,5]{1,0:T(4,128)} %bitcast.7, f32[1,1024]{1,0:T(1,128)} %bitcast.6, s32[8,2,128]{2,1,0:T(2,128)} %halo_hbm.1, f32[512,1024]{1,0:T(8,128)} %bitcast.4, bf16[1024,3072]{1,0:T(8,128)(2,1)} %wqkv_ref.1), custom_call_target="tpu_custom_call" | custom-call | tf_op jit(solution)/shard_map/attention/pallas_call | solution.py:339
  55.3 4.3 %output.1 = f32[512,1024]{1,0:T(8,128)} custom-call(s32[1]{0:T(128)S(6)} %copy.8.counts_hbm.counts_ref, bf16[512,1024]{1,0:T(8,128)(2,1)} %attention.1.att_hbm, f32[512,1024]{1,0:T(8,128)} %bitcast.5, bf16[1024,1024]{1,0:T(8,128)(2,1)} %wout_hbm.1), custom_call_target="tpu_custom_call" | custom-call | tf_op jit(solution)/shard_map/output/pallas_call | solution.py:379
